TPU v7x, 256 devices: a whole 4x4x8 slice. The times are simulated.
256 devices in a mesh: ctx: 8 (over z_hi, core), vocab: 32 (over x, y, z_lo).
Axes of the slice: x: 4, y: 4, z: 8 (z_hi: 4, z_lo: 2; z = z_hi * 2 + z_lo), core: 2. Of those that a mesh axis runs over, the one named last changes fastest.
Arguments:
- hidden: bfloat16 [512, 2, 7168], P('ctx', None, 'vocab'), may hold values from -30 to 30
- head: bfloat16 [7168, 65536], P('ctx', 'vocab'), may hold values from -0.15 to 0.15
- targets: int32 [512, 2], P('ctx'), may hold values from 0 to 65535
- loss_weight: float32 [512, 2], P('ctx'), may hold values from 16 to 256
Outputs:
- token_loss: float32 [512, 2], P('ctx')
- grad_hidden: bfloat16 [512, 2, 7168], P('ctx', None, 'vocab')
All inputs are finite; a program needn't handle non-finite values.
Results may differ from a plain program's by a relative error of at most 0.0046.
Values may be sent and summed in bfloat16 or wider, within the bound.
A program may use at most 64 MiB of HBM per device.

v0:
```python
import jax
import jax.numpy as jnp
from jax import lax
from jax.sharding import PartitionSpec as P


def sent_to_all(x, axis):
    copies = jnp.broadcast_to(x, (lax.axis_size(axis), *x.shape))
    return lax.all_to_all(copies, axis, split_axis=0, concat_axis=0, tiled=True)


def gathered_once(x, axis):
    leaves = jax.tree.leaves(x)
    order = sorted(range(len(leaves)), key=lambda k: -leaves[k].size)
    width = (1, *leaves[order[0]].shape)[-1]
    lines = [
        jnp.pad(leaves[k].reshape(-1), (0, -leaves[k].size % width)).reshape(-1, width)
        for k in order
    ]
    both, at, found = (sent_to_all(jnp.concatenate(lines), axis), 0, {})
    for k, line in zip(order, lines):
        slab = both[:, at : at + len(line)].reshape(len(both), -1)
        found[k] = slab[:, : leaves[k].size].reshape(-1, *leaves[k].shape)
        at += len(line)
    numbers = iter(range(len(leaves)))
    return jax.tree.map(lambda _: found[next(numbers)], x)


def combined_pairwise(pieces, combine):
    while len(jax.tree.leaves(pieces)[0]) > 1:
        pieces = jax.vmap(combine)(
            *(jax.tree.map(lambda part: part[side::2], pieces) for side in (0, 1))
        )
    return jax.tree.map(lambda part: part[0], pieces)


def joined_all(x, axis, combine):
    pieces = gathered_once(x, axis)
    return combined_pairwise(pieces, combine)


def cut_along(x, dim, size):
    lengths = x.shape
    pieces = x.reshape(*lengths[:dim], size, lengths[dim] // size, *lengths[dim + 1 :])
    return jnp.moveaxis(pieces, dim, 0)


def summed_on_arrival(x, axis, dim):
    pieces = cut_along(x, dim, lax.axis_size(axis))
    arrived = lax.all_to_all(pieces, axis, split_axis=0, concat_axis=0, tiled=True)
    return arrived.sum(axis=0)


def combine_stats(first, second):
    first_max, first_sum, first_target = first
    second_max, second_sum, second_target = second
    joined = jnp.maximum(first_max, second_max)
    total = first_sum * jnp.exp(first_max - joined) + second_sum * jnp.exp(second_max - joined)
    return (joined, total, first_target + second_target)


def body(hidden, head, targets, loss_weight):
    group_rows = hidden.shape[0]
    depth_count = hidden.shape[1]
    flat_count = group_rows * depth_count
    ctx_count = lax.axis_size("ctx")
    vocab_count = lax.axis_size("vocab")
    vocab_index = lax.axis_index("vocab")
    vocab_local = head.shape[1]
    flat_hidden = hidden.reshape(flat_count, hidden.shape[2])
    flat_targets = targets.reshape(flat_count)
    flat_weights = loss_weight.reshape(flat_count)
    whole_width = lax.all_gather(flat_hidden, "vocab", axis=1, tiled=True)
    width_slab = lax.all_to_all(whole_width, "ctx", split_axis=1, concat_axis=0, tiled=True)
    logits = lax.psum_scatter(
        jnp.dot(width_slab, head, preferred_element_type=jnp.float32),
        "ctx",
        scatter_dimension=0,
        tiled=True,
    )
    columns = vocab_index * vocab_local + lax.broadcasted_iota(jnp.int32, logits.shape, 1)
    target_hit = columns == flat_targets[:, None]
    local_max = jnp.max(logits, axis=1)
    local_target = jnp.sum(jnp.where(target_hit, logits, 0.0), axis=1)
    local_sum = jnp.sum(jnp.exp(logits - local_max[:, None]), axis=1)
    row_max, sum_exp, target_logit = joined_all(
        (local_max, local_sum, local_target), "vocab", combine_stats
    )
    flat_loss = jnp.log(sum_exp) + row_max - target_logit
    token_loss = flat_loss.reshape(group_rows, depth_count)
    probabilities = jnp.exp(logits - row_max[:, None]) / sum_exp[:, None]
    dlogits = (flat_weights[:, None] * (probabilities - target_hit.astype(jnp.float32))).astype(
        jnp.bfloat16
    )
    grad_slab = lax.dot_general(
        lax.all_gather(dlogits, "ctx", axis=0, tiled=True),
        head,
        (((1,), (1,)), ((), ())),
        preferred_element_type=jnp.float32,
    )
    share_rows = flat_count // vocab_count
    slab_width = grad_slab.shape[1]
    blocks = grad_slab.reshape(ctx_count, vocab_count, share_rows, slab_width)
    reduced = summed_on_arrival(blocks, "vocab", 1).astype(jnp.bfloat16)
    landed = lax.all_to_all(
        lax.all_to_all(reduced, "ctx", split_axis=0, concat_axis=3, tiled=True),
        "vocab",
        split_axis=3,
        concat_axis=1,
        tiled=True,
    )
    grad_out = landed.reshape(group_rows, depth_count, landed.shape[3])
    return (token_loss, grad_out)


def solution(mesh):
    return jax.shard_map(
        body,
        mesh=mesh,
        in_specs=(P("ctx", None, "vocab"), P("ctx", "vocab"), P("ctx", None), P("ctx", None)),
        out_specs=(P("ctx", None), P("ctx", None, "vocab")),
        check_vma=False,
    )
```

profile of v0, /device:TPU:1, one launch (start us, length us, event | category | flops | bytes accessed | tf_op | source)
XLA Modules:
  0.0 565.0 jit_solution(5996300982655620662)
XLA Ops:
  7.2 0.0 all-gather.3.cloned.1.call-start
  7.2 0.9 reshape.54
  8.1 0.7 copy.29
  8.8 0.0 all-gather.3.cloned.1.call-update
  8.9 0.0 reduce-scatter.2.cloned.1.call-start
  8.9 141.3 %all-gather.3.cloned.1.call-done = bf16[128,7168]{0,1:T(8,128)(2,1)} async-done(((bf16[128,224]{0,1:T(8,128)(2,1)}), bf16[128,7168]{0,1:T(8,128)(2,1)}) %all-gather.3.cloned.1.call-update) | async-done | bytes 1835024 | tf_op jit(solution)/shard_map/all_gather | solution.py:73
  150.2 72.8 %all_to_all.62 = bf16[128,8,896]{0,2,1:T(8,128)(2,1)S(1)} all-to-all(bf16[128,8,896]{0,2,1:T(8,128)(2,1)} %bitcast.42), channel_id=1, replica_groups=mesh['ctx'=8,'vocab'=32] {'ctx'}, dimensions={1} | all-to-all | bytes 3670016 | tf_op jit(solution)/shard_map/all_to_all | solution.py:74
  222.9 2.7 copy.30
  225.6 10.3 %fusion.6 = f32[1024,2048]{1,0:T(8,128)} fusion(bf16[1024,896]{1,0:T(8,128)(2,1)} %bitcast.43, bf16[896,2048]{1,0:T(8,128)(2,1)} %param.5), kind=kOutput, calls=%fused_computation.20 | convolution fusion | flops 3758096384 | bytes 13893632 | tf_op jit(solution)/shard_map/dot_general | solution.py:76
  235.9 0.0 copy-start
  236.0 0.0 copy-start.1
  236.0 0.0 reduce-scatter.2.cloned.1.call-update
  236.0 0.6 copy-done
  236.6 0.1 copy.31
  236.7 0.1 eq.10
  236.9 88.8 %reduce-scatter.2.cloned.1.call-done = f32[128,2048]{1,0:T(8,128)} async-done(((f32[1024,2048]{1,0:T(8,128)}), f32[128,2048]{1,0:T(8,128)}) %reduce-scatter.2.cloned.1.call-update) | async-done | bytes 1048592 | tf_op jit(solution)/shard_map/reduce_scatter | solution.py:75
  325.7 1.4 reduce_max.9
  327.0 1.6 exponential_reduce_fusion
  328.6 0.6 broadcast_in_dim.9
  329.3 8.1 %all-to-all-start.1 = ((f32[32,3,128]{2,1,0:T(4,128)}), f32[32,3,128]{2,1,0:T(4,128)S(1)}, u32[]{:S(2)}, u32[]{:S(2)}) async-start(f32[32,3,128]{2,1,0:T(4,128)} %broadcast_in_dim.9), calls=%async_computation.2 | async-start | bytes 131072 | tf_op jit(solution)/shard_map/all_to_all | solution.py:9
  337.4 0.0 all-gather.5.cloned.1.call-start
  337.5 0.0 copy-done.1
  337.5 0.1 copy.34
  337.6 0.1 mul.54
  337.7 6.9 %all-to-all-done.1 = f32[32,3,128]{2,1,0:T(4,128)S(1)} async-done(((f32[32,3,128]{2,1,0:T(4,128)}), f32[32,3,128]{2,1,0:T(4,128)S(1)}, u32[]{:S(2)}, u32[]{:S(2)}) %all-to-all-start.1) | async-done | bytes 49184 | tf_op jit(solution)/shard_map/all_to_all | solution.py:9
  345.2 2.4 fusion.3
  347.6 0.0 all-gather.5.cloned.1.call-update
  347.7 51.8 %all-gather.5.cloned.1.call-done = bf16[1024,2048]{1,0:T(8,128)(2,1)} async-done(((bf16[128,2048]{1,0:T(8,128)(2,1)}), bf16[1024,2048]{1,0:T(8,128)(2,1)}) %all-gather.5.cloned.1.call-update) | async-done | bytes 4194320 | tf_op jit(solution)/shard_map/all_gather | solution.py:96
  399.5 9.7 %fusion.7 = f32[1024,896]{1,0:T(8,128)} fusion(bf16[1024,2048]{1,0:T(8,128)(2,1)} %all-gather.5.cloned.1.call-done, bf16[896,2048]{1,0:T(8,128)(2,1)} %param.5), kind=kOutput, calls=%fused_computation.21 | convolution fusion | flops 3758096384 | bytes 11534336 | tf_op jit(solution)/shard_map/dot_general | solution.py:95
  409.2 5.0 reshape_reshape.3
  414.2 3.1 copy.46
  417.2 52.6 %all_to_all.63 = f32[32,8,1,4,896]{4,3,1,2,0:T(4,128)} all-to-all(f32[32,8,1,4,896]{4,3,1,2,0:T(4,128)S(1)} %bitcast.38), channel_id=1, replica_groups=mesh['ctx'=8,'vocab'=32] {'vocab'}, dimensions={0} | all-to-all | bytes 7340032 | tf_op jit(solution)/shard_map/all_to_all | solution.py:50
  469.9 2.7 reduce_sum.29
  472.5 12.3 %all_to_all.64 = bf16[8,1,4,896]{3,2,1,0:T(4,128)(2,1)S(1)} all-to-all(bf16[8,1,4,896]{3,2,1,0:T(4,128)(2,1)S(1)} %bitcast.45), channel_id=1, replica_groups=mesh['ctx'=8,'vocab'=32] {'ctx'}, dimensions={0} | all-to-all | bytes 114688 | tf_op jit(solution)/shard_map/all_to_all | solution.py:106
  484.8 6.0 %copy.38 = bf16[1,1,4,7168]{2,1,0,3:T(2,128)(2,1)} copy(bf16[1,1,4,7168]{3,2,1,0:T(4,128)(2,1)S(1)} %bitcast.46) | data formatting | bytes 114688 | tf_op jit(solution)/shard_map/all_to_all | solution.py:106
  490.8 0.5 broadcast.6
  491.3 39.8 %reduce.5 = bf16[7168,4]{1,0:T(8,128)(2,1)S(1)} reduce(bf16[7168,1,1,4]{3,2,1,0:T(2,128)(2,1)} %bitcast.40, bf16[]{:T(256)} %broadcast.6), dimensions={1,2}, to_apply=%bitcast.31.reduce_sub_computation | reduce | bytes 114690
  531.1 2.5 reshape.69
  533.6 3.9 all-to-all-start.4
  537.5 0.1 sub.71
  537.6 0.6 copy.41
  538.2 6.5 %all-to-all-done.4 = bf16[32,2,448]{2,1,0:T(2,128)(2,1)S(1)} async-done(((bf16[32,2,448]{2,1,0:T(2,128)(2,1)}), bf16[32,2,448]{2,1,0:T(2,128)(2,1)S(1)}, u32[]{:S(2)}, u32[]{:S(2)}) %all-to-all-start.4) | async-done | bytes 57376 | tf_op jit(solution)/shard_map/all_to_all | solution.py:105
  544.7 5.7 %reshape.70 = bf16[7168,1,1,4]{3,2,1,0:T(2,128)(2,1)} reshape(bf16[32,2,448]{2,1,0:T(2,128)(2,1)S(1)} %all-to-all-done.4) | data formatting | bytes 114688
  550.5 7.1 %copy.39 = bf16[1,1,4,7168]{3,2,1,0:T(4,128)(2,1)S(1)} copy(bf16[1,1,4,7168]{2,1,0,3:T(2,128)(2,1)} %bitcast.39) | data formatting | bytes 114688 | tf_op jit(solution)/shard_map/all_to_all | solution.py:105
  557.6 0.1 all_to_all.55
  557.7 0.1 copy.40
  557.8 0.7 reshape.61
  (36 shorter events, 0.5 us)
Async XLA Ops:
  7.2 143.0 %all-gather.3.cloned.1.call-start = ((), (), s32[]{:S(2)}) async-start(), calls=%async_computation.6 | async-start | bytes 1892352 | tf_op jit(solution)/shard_map/all_gather | solution.py:73
  8.9 316.8 %reduce-scatter.2.cloned.1.call-start = ((), (), s32[]{:S(2)}) async-start(), calls=%async_computation.7 | async-start | bytes 9437184 | tf_op jit(solution)/shard_map/reduce_scatter | solution.py:75
  235.9 0.7 copy-start
  236.0 101.5 %copy-start.1 = (f32[64,2]{0,1:T(2,128)S(1)}, f32[64,2]{0,1:T(2,128)}, u32[]{:S(2)}) copy-start(f32[64,2]{0,1:T(2,128)} %param.7) | copy-start | bytes 1540
  329.3 15.3 %all-to-all-start.1 = ((f32[32,3,128]{2,1,0:T(4,128)}), f32[32,3,128]{2,1,0:T(4,128)S(1)}, u32[]{:S(2)}, u32[]{:S(2)}) async-start(f32[32,3,128]{2,1,0:T(4,128)} %broadcast_in_dim.9), calls=%async_computation.2 | async-start | bytes 131072 | tf_op jit(solution)/shard_map/all_to_all | solution.py:9
  337.4 62.1 %all-gather.5.cloned.1.call-start = ((), (), s32[]{:S(2)}) async-start(), calls=%async_computation.8 | async-start | bytes 4718592 | tf_op jit(solution)/shard_map/all_gather | solution.py:96
  533.6 11.1 %all-to-all-start.4 = ((bf16[32,2,448]{2,1,0:T(2,128)(2,1)}), bf16[32,2,448]{2,1,0:T(2,128)(2,1)S(1)}, u32[]{:S(2)}, u32[]{:S(2)}) async-start(bf16[32,2,448]{2,1,0:T(2,128)(2,1)} %reshape.69), calls=%async_computation.5 | async-start | bytes 131072 | tf_op jit(solution)/shard_map/all_to_all | solution.py:105
Sparse Core Ops, SparseCore 0:
  10.3 139.7 all-gather.2
  236.1 89.5 reduce-scatter.1
  347.8 51.6 all-gather.4
where the time goes:
time: 566 us; the launch traced here: 565 us
  waiting for transfers between devices  295 us (52%)
  blocking collectives  138 us (24%)
  other arithmetic  47.9 us (8%)
  local copies, waits for them, and re-layouts  38.1 us (7%)
  matrix products  20 us (4%)
  between operations  13.9 us (2%)
  starting transfers between devices  12.1 us (2%)
    all_gather x1, waiting for transfers between devices, body(): whole_width = lax.all_gather(flat_hidden, 'vocab', axis=1, tiled=True)  141 us
    reduce_scatter x1, waiting for transfers between devices, body(): lax.psum_scatter(jnp.dot(width_slab, head, preferred_element_type=jnp.flo...  88.8 us
    all_to_all x1, blocking collectives, body(): lax.all_to_all(whole_width, 'ctx', split_axis=1, concat_axis=0, tiled=True)  72.8 us
    all_to_all x1, blocking collectives, summed_on_arrival(): lax.all_to_all(pieces, axis, split_axis=0, concat_axis=0, tiled=True)  52.6 us
    all_gather x1, waiting for transfers between devices, body(): lax.all_gather(dlogits, 'ctx', axis=0, tiled=True)  51.8 us
    unnamed x1, other arithmetic  39.8 us
    all_to_all x1, blocking collectives, body(): lax.all_to_all(reduced, 'ctx', split_axis=0, concat_axis=3, tiled=True)  12.3 us
  transfers between devices with their start and end apart: 5, of which 5 were waited for; matrix products, arithmetic and copies ran while one was open for 0% of the time, Pallas kernels for 0%

commit v1 on v0

--- a/solution.py
+++ b/solution.py
@@ -70,7 +70,12 @@
     flat_hidden = hidden.reshape(flat_count, hidden.shape[2])
     flat_targets = targets.reshape(flat_count)
     flat_weights = loss_weight.reshape(flat_count)
-    whole_width = lax.all_gather(flat_hidden, "vocab", axis=1, tiled=True)
+    whole_width = jnp.concatenate(
+        lax.all_to_all(
+            jnp.stack([flat_hidden for _ in range(lax.axis_size("vocab"))]), "vocab", 0, 0
+        ),
+        axis=1,
+    )
     width_slab = lax.all_to_all(whole_width, "ctx", split_axis=1, concat_axis=0, tiled=True)
     logits = lax.psum_scatter(
         jnp.dot(width_slab, head, preferred_element_type=jnp.float32),

time: 566 us -> 439 us (0.78)
  waiting for transfers between devices: 295 us -> 153 us
  blocking collectives: 138 us -> 153 us
    all_gather x1 -> x0, waiting for transfers between devices: 141 us -> none  [body(): whole_width = lax.all_gather(flat_hidden, 'vocab', axis=1, tiled=True)]
    all_to_all x0 -> x1, blocking collectives: none -> 34.2 us  [body(): lax.all_to_all(jnp.stack([flat_hidden for _ in range(lax.axis_size('vocab...]
    all_to_all x1, blocking collectives: 72.8 us -> 54.1 us  [body(): lax.all_to_all(whole_width, 'ctx', split_axis=1, concat_axis=0, tiled=True)]
  transfers between devices with their start and end apart: 5 -> 4, of which waited for: 5 -> 4; matrix products, arithmetic and copies ran while one was open for 0% -> 0% of each run, Pallas kernels for 0% -> 0%
where the time goes in v1:
time: 439 us
  blocking collectives  153 us (35%)
  waiting for transfers between devices  153 us (35%)
  other arithmetic  47.9 us (11%)
  local copies, waits for them, and re-layouts  37.7 us (9%)
  matrix products  20 us (5%)
  between operations  14.2 us (3%)
  starting transfers between devices  12.2 us (3%)
    reduce_scatter x1, waiting for transfers between devices, body(): lax.psum_scatter(jnp.dot(width_slab, head, preferred_element_type=jnp.flo...  87.8 us
    all_to_all x1, blocking collectives, body(): lax.all_to_all(whole_width, 'ctx', split_axis=1, concat_axis=0, tiled=True)  54.1 us
    all_to_all x1, blocking collectives, summed_on_arrival(): lax.all_to_all(pieces, axis, split_axis=0, concat_axis=0, tiled=True)  52.6 us
    all_gather x1, waiting for transfers between devices, body(): lax.all_gather(dlogits, 'ctx', axis=0, tiled=True)  51.8 us
    unnamed x1, other arithmetic  39.8 us
    all_to_all x1, blocking collectives, body(): lax.all_to_all(jnp.stack([flat_hidden for _ in range(lax.axis_size('vocab...  34.2 us
    all_to_all x1, blocking collectives, body(): lax.all_to_all(reduced, 'ctx', split_axis=0, concat_axis=3, tiled=True)  12.5 us
    dot_general x1, matrix products, body(): jnp.dot(width_slab, head, preferred_element_type=jnp.float32)  10.3 us
  transfers between devices with their start and end apart: 4, of which 4 were waited for; matrix products, arithmetic and copies ran while one was open for 0% of the time, Pallas kernels for 0%

profile of v1, /device:TPU:1, one launch (start us, length us, event | category | flops | bytes accessed | tf_op | source)
XLA Modules:
  0.0 438.5 jit_solution(13208148441567297351)
XLA Ops:
  7.2 0.0 reduce-scatter.2.cloned.1.call-start
  7.2 0.9 stack_reshape.2
  8.1 0.1 copy.32
  8.2 0.2 stack.3
  8.5 34.2 %all_to_all.67 = bf16[32,128,224]{1,2,0:T(8,128)(2,1)S(1)} all-to-all(bf16[32,128,224]{1,2,0:T(8,128)(2,1)S(1)} %stack.3), channel_id=1, replica_groups=mesh['ctx'=8,'vocab'=32] {'vocab'}, dimensions={0} | all-to-all | bytes 3670016 | tf_op jit(solution)/shard_map/all_to_all | solution.py:74
  42.6 54.1 %all_to_all.68 = bf16[128,8,896]{0,2,1:T(8,128)(2,1)S(1)} all-to-all(bf16[128,8,896]{0,2,1:T(8,128)(2,1)S(1)} %bitcast.43), channel_id=1, replica_groups=mesh['ctx'=8,'vocab'=32] {'ctx'}, dimensions={1} | all-to-all | bytes 3670016 | tf_op jit(solution)/shard_map/all_to_all | solution.py:79
  96.7 2.7 copy.33
  99.4 10.3 %fusion.6 = f32[1024,2048]{1,0:T(8,128)} fusion(bf16[1024,896]{1,0:T(8,128)(2,1)} %bitcast.45, bf16[896,2048]{1,0:T(8,128)(2,1)} %param.5), kind=kOutput, calls=%fused_computation.20 | convolution fusion | flops 3758096384 | bytes 13893632 | tf_op jit(solution)/shard_map/dot_general | solution.py:81
  109.8 0.0 copy-start
  109.8 0.0 copy-start.1
  109.8 0.0 reduce-scatter.2.cloned.1.call-update
  109.8 0.6 copy-done
  110.4 0.1 copy.34
  110.5 0.1 eq.10
  110.7 87.8 %reduce-scatter.2.cloned.1.call-done = f32[128,2048]{1,0:T(8,128)} async-done(((f32[1024,2048]{1,0:T(8,128)}), f32[128,2048]{1,0:T(8,128)}) %reduce-scatter.2.cloned.1.call-update) | async-done | bytes 1048592 | tf_op jit(solution)/shard_map/reduce_scatter | solution.py:80
  198.5 1.4 reduce_max.9
  199.9 1.6 exponential_reduce_fusion
  201.5 0.6 broadcast_in_dim.9
  202.1 8.3 %all-to-all-start.2 = ((f32[32,3,128]{2,1,0:T(4,128)}), f32[32,3,128]{2,1,0:T(4,128)S(1)}, u32[]{:S(2)}, u32[]{:S(2)}) async-start(f32[32,3,128]{2,1,0:T(4,128)} %broadcast_in_dim.9), calls=%async_computation.3 | async-start | bytes 131072 | tf_op jit(solution)/shard_map/all_to_all | solution.py:9
  210.4 0.0 all-gather.2.cloned.1.call-start
  210.5 0.0 copy-done.1
  210.5 0.1 copy.37
  210.6 0.1 mul.54
  210.7 6.9 %all-to-all-done.2 = f32[32,3,128]{2,1,0:T(4,128)S(1)} async-done(((f32[32,3,128]{2,1,0:T(4,128)}), f32[32,3,128]{2,1,0:T(4,128)S(1)}, u32[]{:S(2)}, u32[]{:S(2)}) %all-to-all-start.2) | async-done | bytes 49184 | tf_op jit(solution)/shard_map/all_to_all | solution.py:9
  218.2 2.4 fusion.3
  220.7 0.0 all-gather.2.cloned.1.call-update
  220.7 51.8 %all-gather.2.cloned.1.call-done = bf16[1024,2048]{1,0:T(8,128)(2,1)} async-done(((bf16[128,2048]{1,0:T(8,128)(2,1)}), bf16[1024,2048]{1,0:T(8,128)(2,1)}) %all-gather.2.cloned.1.call-update) | async-done | bytes 4194320 | tf_op jit(solution)/shard_map/all_gather | solution.py:101
  272.4 9.7 %fusion.7 = f32[1024,896]{1,0:T(8,128)} fusion(bf16[1024,2048]{1,0:T(8,128)(2,1)} %all-gather.2.cloned.1.call-done, bf16[896,2048]{1,0:T(8,128)(2,1)} %param.5), kind=kOutput, calls=%fused_computation.21 | convolution fusion | flops 3758096384 | bytes 11534336 | tf_op jit(solution)/shard_map/dot_general | solution.py:100
  282.1 5.0 %reshape_reshape.3 = f32[8,32,1,4,896]{4,3,1,0,2:T(4,128)} reshape(f32[1024,896]{1,0:T(8,128)} %fusion.7) | data formatting | bytes 7340032 | tf_op jit(solution)/shard_map/reshape;reshape | solution.py:44
  287.1 3.1 copy.49
  290.2 52.6 %all_to_all.69 = f32[32,8,1,4,896]{4,3,1,2,0:T(4,128)} all-to-all(f32[32,8,1,4,896]{4,3,1,2,0:T(4,128)S(1)} %bitcast.40), channel_id=1, replica_groups=mesh['ctx'=8,'vocab'=32] {'vocab'}, dimensions={0} | all-to-all | bytes 7340032 | tf_op jit(solution)/shard_map/all_to_all | solution.py:50
  342.8 2.7 reduce_sum.29
  345.5 12.5 %all_to_all.70 = bf16[8,1,4,896]{3,2,1,0:T(4,128)(2,1)S(1)} all-to-all(bf16[8,1,4,896]{3,2,1,0:T(4,128)(2,1)S(1)} %bitcast.47), channel_id=1, replica_groups=mesh['ctx'=8,'vocab'=32] {'ctx'}, dimensions={0} | all-to-all | bytes 114688 | tf_op jit(solution)/shard_map/all_to_all | solution.py:111
  358.0 6.0 %copy.41 = bf16[1,1,4,7168]{2,1,0,3:T(2,128)(2,1)} copy(bf16[1,1,4,7168]{3,2,1,0:T(4,128)(2,1)S(1)} %bitcast.48) | data formatting | bytes 114688 | tf_op jit(solution)/shard_map/all_to_all | solution.py:111
  364.0 0.5 broadcast.7
  364.5 39.8 %reduce.5 = bf16[7168,4]{1,0:T(8,128)(2,1)S(1)} reduce(bf16[7168,1,1,4]{3,2,1,0:T(2,128)(2,1)} %bitcast.42, bf16[]{:T(256)} %broadcast.7), dimensions={1,2}, to_apply=%bitcast.33.reduce_sub_computation | reduce | bytes 114690
  404.3 2.5 reshape.73
  406.8 3.9 all-to-all-start.5
  410.6 0.1 sub.71
  410.8 0.6 copy.44
  411.4 6.5 %all-to-all-done.5 = bf16[32,2,448]{2,1,0:T(2,128)(2,1)S(1)} async-done(((bf16[32,2,448]{2,1,0:T(2,128)(2,1)}), bf16[32,2,448]{2,1,0:T(2,128)(2,1)S(1)}, u32[]{:S(2)}, u32[]{:S(2)}) %all-to-all-start.5) | async-done | bytes 57376 | tf_op jit(solution)/shard_map/all_to_all | solution.py:110
  417.9 5.8 %reshape.74 = bf16[7168,1,1,4]{3,2,1,0:T(2,128)(2,1)} reshape(bf16[32,2,448]{2,1,0:T(2,128)(2,1)S(1)} %all-to-all-done.5) | data formatting | bytes 114688
  423.7 7.1 %copy.42 = bf16[1,1,4,7168]{3,2,1,0:T(4,128)(2,1)S(1)} copy(bf16[1,1,4,7168]{2,1,0,3:T(2,128)(2,1)} %bitcast.41) | data formatting | bytes 114688 | tf_op jit(solution)/shard_map/all_to_all | solution.py:110
  430.8 0.1 all_to_all.59
  431.0 0.1 copy.43
  431.0 0.7 reshape.65
  (36 shorter events, 0.5 us)
Async XLA Ops:
  7.2 191.4 %reduce-scatter.2.cloned.1.call-start = ((), (), s32[]{:S(2)}) async-start(), calls=%async_computation.7 | async-start | bytes 9437184 | tf_op jit(solution)/shard_map/reduce_scatter | solution.py:80
  109.8 0.7 copy-start
  109.8 100.7 %copy-start.1 = (f32[64,2]{0,1:T(2,128)S(1)}, f32[64,2]{0,1:T(2,128)}, u32[]{:S(2)}) copy-start(f32[64,2]{0,1:T(2,128)} %param.7) | copy-start | bytes 1540
  202.1 15.5 %all-to-all-start.2 = ((f32[32,3,128]{2,1,0:T(4,128)}), f32[32,3,128]{2,1,0:T(4,128)S(1)}, u32[]{:S(2)}, u32[]{:S(2)}) async-start(f32[32,3,128]{2,1,0:T(4,128)} %broadcast_in_dim.9), calls=%async_computation.3 | async-start | bytes 131072 | tf_op jit(solution)/shard_map/all_to_all | solution.py:9
  210.4 62.0 %all-gather.2.cloned.1.call-start = ((), (), s32[]{:S(2)}) async-start(), calls=%async_computation.8 | async-start | bytes 4718592 | tf_op jit(solution)/shard_map/all_gather | solution.py:101
  406.8 11.1 %all-to-all-start.5 = ((bf16[32,2,448]{2,1,0:T(2,128)(2,1)}), bf16[32,2,448]{2,1,0:T(2,128)(2,1)S(1)}, u32[]{:S(2)}, u32[]{:S(2)}) async-start(bf16[32,2,448]{2,1,0:T(2,128)(2,1)} %reshape.73), calls=%async_computation.6 | async-start | bytes 131072 | tf_op jit(solution)/shard_map/all_to_all | solution.py:110
Sparse Core Ops, SparseCore 0:
  109.9 88.5 reduce-scatter.1
  220.8 51.5 all-gather.1
